TPU v7x, 256 devices: a whole 4x4x8 slice. The times are simulated.
256 devices in a mesh: inst: 8 (over x, y_lo), space: 32 (over z, y_hi, core).
Axes of the slice: x: 4, y: 4 (y_hi: 2, y_lo: 2; y = y_hi * 2 + y_lo), z: 8, core: 2. Of those that a mesh axis runs over, the one named last changes fastest.
Arguments:
- adjoint: float32 [8, 5, 256, 64, 128], P('inst', None, 'space'), may hold values from -6 to 6
- source: float32 [8, 5, 256, 64, 128], P('inst', None, 'space'), may hold values from -6 to 6
- viscosity: float32 [256, 64, 128], P('space'), may hold values from 0.2 to 2
- kappa: float32 [5], replicated, may hold values from 0.5 to 2
- coupling: float32 [5, 5], replicated, may hold values from -2.4 to 2.4
- bc_flags: int32 [5, 3], replicated, may hold values 0 or 1
- inst_map: int32 [8], replicated, may hold values from 0 to 7, each once
Outputs:
- residual: float32 [8, 5, 256, 64, 128], P('inst', None, 'space')
Inputs may be any that keep to these rules, and one draw needn't show every extreme that they name: `inst_map`: a permutation of 0 to 7. `bc_flags`: 1 marks a face of zero normal flux, 0 a face held at zero.
All inputs are finite; a program needn't handle non-finite values.
Results may differ from a plain program's by a relative error of at most 0.0001.
Values sent between devices are 32-bit elements; how exact they have to be, the bound alone decides.
A program may use at most 128 MiB of HBM per device.

v0:
```python
import jax
import jax.numpy as jnp
from jax import lax
from jax.sharding import PartitionSpec as P


def with_halo(block, sides, width):
    for axis, dim in sides:
        count = lax.axis_size(axis)
        forward = [(i, i + 1) for i in range(count - 1)]
        forward.append((count - 1, 0))
        backward = [(target, source) for source, target in forward]
        low = lax.ppermute(
            lax.slice_in_dim(block, block.shape[dim] - width, None, axis=dim), axis, forward
        )
        high = lax.ppermute(lax.slice_in_dim(block, 0, width, axis=dim), axis, backward)
        block = jnp.concatenate([low, block, high], axis=dim)
    return block


def spectral_matrix(labels, slots):
    offset = labels[:, None] - labels[None, :]
    parity = (1 - 2 * (jnp.abs(offset) % 2)).astype(jnp.float32)
    sines = jnp.sin(jnp.pi * offset.astype(jnp.float32) / slots)
    safe = jnp.where(offset == 0, jnp.float32(1.0), sines)
    return jnp.where(offset == 0, jnp.float32(0.0), 0.5 * parity / safe)


def mode_tables(points):
    indices = jnp.arange(points, dtype=jnp.int32)
    product = indices[:, None] * indices[None, :] % points
    angles = 2.0 * jnp.pi * product.astype(jnp.float32) / points
    return (jnp.cos(angles), jnp.sin(angles))


def cycle_response(points, cycle_index, near):
    indices = jnp.arange(points, dtype=jnp.int32)
    wave_number = jnp.minimum(indices, points - indices)
    cutoff = jnp.maximum(4, points * (cycle_index + 1) // (2 * near))
    return (wave_number[None, :] < cutoff[:, None]).astype(jnp.float32)


def smooth_cycles(pencil, first_cycle, near):
    points = pencil.shape[1]
    cycles = pencil.shape[2]
    cosines, sines_table = mode_tables(points)
    cycle_index = first_cycle + jnp.arange(cycles, dtype=jnp.int32)
    response = (cycle_response(points, cycle_index, near).T / points)[None, :, :, None]
    coef_cos = jnp.einsum("tk,ftrx->fkrx", cosines, pencil, precision=lax.Precision.HIGHEST)
    coef_sin = jnp.einsum("tk,ftrx->fkrx", sines_table, pencil, precision=lax.Precision.HIGHEST)
    smoothed = jnp.einsum(
        "tk,fkrx->ftrx", cosines, coef_cos * response, precision=lax.Precision.HIGHEST
    )
    smoothed = smoothed + jnp.einsum(
        "tk,fkrx->ftrx", sines_table, coef_sin * response, precision=lax.Precision.HIGHEST
    )
    weights = jnp.maximum(1.0 - cycle_index.astype(jnp.float32) / near, 0.0)[None, None, :, None]
    return pencil + weights * (smoothed - pencil)


def viscous(center, nbr_up, nbr_dn, visc, visc_up, visc_dn, kappa, flags):
    cycles = center.shape[2]
    cells_x = center.shape[3]
    cycle_weight = (1.0 / (jnp.arange(cycles, dtype=jnp.float32) + 1.0))[None, :, None]
    theta = cycle_weight * (
        0.5 * (visc + visc_up) * (center - nbr_up) + 0.5 * (visc + visc_dn) * (center - nbr_dn)
    )
    face_r = 0.5 * (visc[:, :-1, :] + visc[:, 1:, :])
    flux_r = face_r * (center[:, :, :-1, :] - center[:, :, 1:, :])
    radial = jnp.pad(flux_r, ((0, 0), (0, 0), (0, 1), (0, 0))) - jnp.pad(
        flux_r, ((0, 0), (0, 0), (1, 0), (0, 0))
    )
    face_x = 0.5 * (visc[:, :, :-1] + visc[:, :, 1:])
    flux_x = face_x * (center[:, :, :, :-1] - center[:, :, :, 1:])
    axial = jnp.pad(flux_x, ((0, 0), (0, 0), (0, 0), (0, 1))) - jnp.pad(
        flux_x, ((0, 0), (0, 0), (0, 0), (1, 0))
    )
    open_faces = (1 - flags).astype(jnp.float32)
    outer = open_faces[:, 2][:, None, None, None] * visc[None, :, -1:, :] * center[:, :, -1:, :]
    outer = jnp.pad(outer, ((0, 0), (0, 0), (cycles - 1, 0), (0, 0)))
    inflow = open_faces[:, 0][:, None, None, None] * visc[None, :, :, :1] * center[:, :, :, :1]
    inflow = jnp.pad(inflow, ((0, 0), (0, 0), (0, 0), (0, cells_x - 1)))
    outflow = open_faces[:, 1][:, None, None, None] * visc[None, :, :, -1:] * center[:, :, :, -1:]
    outflow = jnp.pad(outflow, ((0, 0), (0, 0), (0, 0), (cells_x - 1, 0)))
    return kappa[:, None, None, None] * (theta + radial + axial + outer + inflow + outflow)


def body(adjoint, source, viscosity, kappa, coupling, bc_flags, inst_map):
    slots = lax.axis_size("inst")
    own_slot = lax.axis_index("inst")
    matrix = spectral_matrix(inst_map, slots)
    center = adjoint[0]
    column = lax.dynamic_slice_in_dim(matrix, own_slot, 1, 1)[:, 0]
    spectral = jnp.tensordot(
        column,
        lax.all_gather(adjoint, "inst", axis=0, tiled=True),
        axes=1,
        precision=lax.Precision.HIGHEST,
    )
    stacked = jnp.concatenate([center, viscosity[None]], axis=0)
    padded = with_halo(stacked, (("space", 1),), 1)
    fields = center.shape[0]
    diffused = viscous(
        center,
        padded[:fields, 2:],
        padded[:fields, :-2],
        viscosity,
        padded[fields, 2:],
        padded[fields, :-2],
        kappa,
        bc_flags,
    )
    coupled = jnp.einsum("gf,gtrx->ftrx", coupling, center, precision=lax.Precision.HIGHEST)
    pre = source[0] + coupled + diffused + spectral
    total_cycles = pre.shape[2]
    near = total_cycles // 2
    pencil = lax.all_to_all(pre, "space", split_axis=2, concat_axis=1, tiled=True)
    first_cycle = lax.axis_index("space") * pencil.shape[2]
    result = smooth_cycles(pencil, first_cycle, near)
    residual = lax.all_to_all(result, "space", split_axis=1, concat_axis=2, tiled=True)
    return residual[None]


def solution(mesh):
    return jax.shard_map(
        body,
        mesh=mesh,
        in_specs=(
            P("inst", None, "space", None, None),
            P("inst", None, "space", None, None),
            P("space", None, None),
            P(),
            P(),
            P(),
            P(),
        ),
        out_specs=P("inst", None, "space", None, None),
        check_vma=False,
    )
```

profile of v0, /device:TPU:4, one launch (start us, length us, event | category | flops | bytes accessed | tf_op | source)
XLA Modules:
  0.0 363.8 jit_solution(16795134154637012902)
XLA Ops:
  6.5 0.0 copy-start
  6.5 0.0 copy-start.1
  6.5 0.0 all-gather.2.cloned.1.call-start
  6.5 0.7 all-gather.2.cloned.1.call-update
  7.3 0.6 copy-done.1
  7.9 1.6 fusion.36
  9.4 0.0 collective-permute-start.1
  9.4 7.9 %collective-permute-start = (f32[6,1,64,128]{3,2,1,0:T(8,128)}, f32[6,1,64,128]{3,2,1,0:T(8,128)}, u32[]{:S(2)}, u32[]{:S(2)}) collective-permute-start(f32[6,1,64,128]{3,2,1,0:T(8,128)} %get-tuple-element.7), channel_id=1, source_target_pairs={{1,0},{2,1},{3,2},{4,3},{5,4},{6,5},{7,6},{8,7},{9,8},{10,9},{11,1... | collective-permute-start | bytes 589832 | tf_op jit(solution)/shard_map/ppermute | solution.py:16
  17.4 0.8 copy.120
  18.2 0.8 slice.88
  18.9 1.9 fusion.78
  20.8 0.0 copy-start.11
  20.8 1.1 copy.102
  21.9 1.1 copy.103
  23.0 0.0 copy-start.2
  23.0 1.2 pad_maximum_fusion
  24.2 0.0 copy-done.11
  24.3 0.1 slice_multiply_fusion.2
  24.3 0.0 copy-done.2
  24.4 0.1 add_multiply_fusion
  24.5 1.6 fusion.14
  26.1 2.0 fusion.2
  28.1 0.0 copy-start.10
  28.1 3.7 %slice_multiply_fusion.1 = (f32[5,8,64,1]{3,0,2,1:T(8,128)}, f32[5,8,64,1]{3,0,2,1:T(8,128)}) fusion(f32[5,8,64,128]{3,0,2,1:T(8,128)S(1)} %bitcast.91, f32[8,64]{1,0:T(8,128)S(1)} %bitcast.107, f32[5]{0:T(128)S(1)} %get-tuple-element.15, f32[8,64]{1,0:T(8,128)S(1)} %bitcast.108, f32[5]{0:T(128)S(1)} %get-tuple-element.14), kind=kLoop, calls=%fused_computation.6 | loop fusion | flops 10240 | bytes 45096 | tf_op jit(solution)/shard_map/mul | solution.py:81
  31.8 0.0 copy-done.10
  31.8 0.1 fusion.47
  31.9 0.0 collective-permute-done.1
  31.9 1.0 copy_dynamic-update-slice_fusion.1
  33.0 0.9 copy_dynamic-update-slice_fusion
  33.9 0.0 copy-start.9
  33.9 0.3 slice.100
  34.2 0.0 collective-permute-done
  34.2 0.9 add_multiply_fusion.2
  35.1 0.3 copy-done.9
  35.4 1.1 fusion.22
  36.5 0.0 copy-start.12
  36.5 189.8 %all-gather.2.cloned.1.call-done = f32[8,5,8,64,128]{4,3,2,1,0:T(8,128)} async-done(((f32[1,5,8,64,128]{4,3,2,1,0:T(8,128)}), f32[8,5,8,64,128]{4,3,2,1,0:T(8,128)}) %all-gather.2.cloned.1.call-update) | async-done | bytes 10485776 | tf_op jit(solution)/shard_map/all_gather | solution.py:96
  226.3 0.0 copy-start.3
  226.3 19.2 %fusion = f32[1,5,8,64,128]{4,0,3,2,1:T(1,128)S(1)} fusion(f32[8,5,8,64,128]{4,3,2,1,0:T(8,128)} %all-gather.2.cloned.1.call-done, f32[8,8]{0,1:T(8,128)S(1)} %fusion.47, s32[]{:T(128)S(6)} %select_n.41), kind=kOutput, calls=%fused_computation | convolution fusion | flops 31457280 | bytes 11796996 | tf_op jit(solution)/shard_map/dot_general | solution.py:94
  245.6 0.0 copy-done
  245.6 0.0 copy-done.12
  245.6 0.0 copy-done.3
  245.6 0.0 copy-done.4
  245.6 0.0 copy-done.5
  245.6 0.0 copy-done.6
  245.6 0.0 copy-done.8
  245.6 8.9 %fusion.13 = f32[5,8,64,128]{3,0,2,1:T(8,128)S(1)} fusion(f32[6,9,64,128]{3,0,2,1:T(8,128)} %copy-done.9, f32[1,5,8,64,128]{4,0,3,2,1:T(1,128)S(1)} %fusion, f32[5,8,64,128]{3,2,1,0:T(8,128)S(1)} %fusion.22, f32[1,5,8,64,128]{4,3,2,1,0:T(8,128)S(1)} %copy-done.8, f32[5,8,64,1]{3,0,2,1:T(8,128)S(1)} %copy-done.5, f32[5,8,64,1]{3,0,2,1:T(8,128)S(1)} %copy-done.4, ...), kind=kOutput, calls=%fused_computation.20 | convolution fusion | flops 24576000 | bytes 17830912 | tf_op jit(solution)/shard_map/gf,gtrx->ftrx/dot_general | solution.py:113
  254.5 1.8 copy.79
  256.4 7.6 %all-to-all-start = ((f32[5,8,64,128]{3,1,0,2:T(8,128)}), f32[5,8,64,128]{3,1,0,2:T(8,128)S(1)}, u32[]{:S(2)}, u32[]{:S(2)}) async-start(f32[5,8,64,128]{3,1,0,2:T(8,128)} %copy.79), calls=%async_computation | async-start | bytes 2621440 | tf_op jit(solution)/shard_map/all_to_all | solution.py:117
  264.0 0.1 compare_select_fusion
  264.1 33.9 %all-to-all-done = f32[5,8,64,128]{3,1,0,2:T(8,128)S(1)} async-done(((f32[5,8,64,128]{3,1,0,2:T(8,128)}), f32[5,8,64,128]{3,1,0,2:T(8,128)S(1)}, u32[]{:S(2)}, u32[]{:S(2)}) %all-to-all-start) | async-done | bytes 1310752 | tf_op jit(solution)/shard_map/all_to_all | solution.py:117
  298.0 1.2 copy.121
  299.1 3.2 fusion.16
  302.3 4.2 %fusion.15 = f32[5,256,2,128]{1,3,2,0:T(8,128)} fusion(f32[256,2]{0,1:T(2,128)S(1)} %compare_select_fusion, f32[5,32,8,2,128]{4,2,0,3,1:T(8,128)S(1)} %bitcast.102), kind=kOutput, calls=%fused_computation.30 | convolution fusion | flops 1007878144 | bytes 2623488 | tf_op jit(solution)/shard_map/tk,ftrx->fkrx/dot_general | solution.py:50
  306.5 1.7 copy.85
  308.2 0.0 copy-start.7
  308.2 2.2 fusion.30
  310.4 0.0 copy-done.7
  310.4 2.3 fusion.20
  312.7 1.3 copy.86
  314.0 41.2 %all_to_all.33 = f32[5,256,2,128]{3,2,0,1:T(2,128)S(1)} all-to-all(f32[5,256,2,128]{3,2,0,1:T(2,128)S(1)} %copy.86), channel_id=1, replica_groups=mesh['inst'=8,'space'=32] {'space'}, dimensions={1} | all-to-all | bytes 2621440 | tf_op jit(solution)/shard_map/all_to_all | solution.py:120
  355.2 0.1 copy.122
  355.3 0.1 copy.88
  355.4 1.3 copy.89
  (11 shorter events, 0.1 us)
Async XLA Ops:
  6.5 239.0 %copy-start = (f32[5,5]{1,0:T(8,128)S(1)}, f32[5,5]{1,0:T(8,128)}, u32[]{:S(2)}) copy-start(f32[5,5]{1,0:T(8,128)} %param.11) | copy-start | bytes 304
  6.5 1.3 copy-start.1
  6.5 219.8 %all-gather.2.cloned.1.call-start = ((), (), s32[]{:S(2)}) async-start(), calls=%async_computation.2 | async-start | bytes 11796480 | tf_op jit(solution)/shard_map/all_gather | solution.py:96
  9.4 22.5 %collective-permute-start.1 = (f32[6,1,64,128]{3,2,1,0:T(8,128)}, f32[6,1,64,128]{3,2,1,0:T(8,128)}, u32[]{:S(2)}, u32[]{:S(2)}) collective-permute-start(f32[6,1,64,128]{3,2,1,0:T(8,128)} %get-tuple-element.8), channel_id=1, source_target_pairs={{0,1},{1,2},{2,3},{3,4},{4,5},{5,6},{6,7},{7,8},{8,9},{9,10},{10,1... | collective-permute-start | bytes 589832 | tf_op jit(solution)/shard_map/ppermute | solution.py:13
  9.4 24.8 %collective-permute-start = (f32[6,1,64,128]{3,2,1,0:T(8,128)}, f32[6,1,64,128]{3,2,1,0:T(8,128)}, u32[]{:S(2)}, u32[]{:S(2)}) collective-permute-start(f32[6,1,64,128]{3,2,1,0:T(8,128)} %get-tuple-element.7), channel_id=1, source_target_pairs={{1,0},{2,1},{3,2},{4,3},{5,4},{6,5},{7,6},{8,7},{9,8},{10,9},{11,1... | collective-permute-start | bytes 589832 | tf_op jit(solution)/shard_map/ppermute | solution.py:16
  20.8 3.4 copy-start.11
  23.0 1.4 copy-start.2
  28.1 3.7 %copy-start.10 = (s32[8]{0:T(128)S(1)}, s32[8]{0:T(128)}, u32[]{:S(2)}) copy-start(s32[8]{0:T(128)} %param.13) | copy-start | bytes 100
  33.9 1.5 copy-start.9
  36.5 209.1 %copy-start.12 = (f32[5]{0:T(128)S(1)}, f32[5]{0:T(128)}, u32[]{:S(2)}) copy-start(f32[5]{0:T(128)} %param.10) | copy-start | bytes 64
  226.3 19.3 %copy-start.3 = (f32[5,8,64,127]{3,0,2,1:T(8,128)S(1)}, f32[5,8,64,127]{3,0,2,1:T(8,128)}, u32[]{:S(2)}) copy-start(f32[5,8,64,127]{3,0,2,1:T(8,128)} %fusion.2) | copy-start | bytes 3901444
  226.3 19.3 %copy-start.4 = (f32[5,8,64,1]{3,0,2,1:T(8,128)S(1)}, f32[5,8,64,1]{3,0,2,1:T(8,128)}, u32[]{:S(2)}) copy-start(f32[5,8,64,1]{3,0,2,1:T(8,128)} %get-tuple-element.5) | copy-start | bytes 30724
  226.3 19.3 %copy-start.5 = (f32[5,8,64,1]{3,0,2,1:T(8,128)S(1)}, f32[5,8,64,1]{3,0,2,1:T(8,128)}, u32[]{:S(2)}) copy-start(f32[5,8,64,1]{3,0,2,1:T(8,128)} %get-tuple-element.6) | copy-start | bytes 30724
  226.3 19.3 %copy-start.6 = (f32[5,8,63,128]{3,0,2,1:T(8,128)S(1)}, f32[5,8,63,128]{3,0,2,1:T(8,128)}, u32[]{:S(2)}) copy-start(f32[5,8,63,128]{3,0,2,1:T(8,128)} %fusion.14) | copy-start | bytes 3870724
  226.3 19.3 %copy-start.8 = (f32[1,5,8,64,128]{4,3,2,1,0:T(8,128)S(1)}, f32[1,5,8,64,128]{4,3,2,1,0:T(8,128)}, u32[]{:S(2)}) copy-start(f32[1,5,8,64,128]{4,3,2,1,0:T(8,128)} %param.8) | copy-start | bytes 3932164
  256.4 41.6 %all-to-all-start = ((f32[5,8,64,128]{3,1,0,2:T(8,128)}), f32[5,8,64,128]{3,1,0,2:T(8,128)S(1)}, u32[]{:S(2)}, u32[]{:S(2)}) async-start(f32[5,8,64,128]{3,1,0,2:T(8,128)} %copy.79), calls=%async_computation | async-start | bytes 2621440 | tf_op jit(solution)/shard_map/all_to_all | solution.py:117
  308.2 2.2 copy-start.7
Sparse Core Ops, SparseCore 0:
  9.1 217.1 all-gather.1
where the time goes:
time: 368 us; the launch traced here: 364 us
  waiting for transfers between devices  224 us (61%)
  blocking collectives  41.2 us (11%)
  matrix products  40 us (11%)
  local copies, waits for them, and re-layouts  16.2 us (4%)
  starting transfers between devices  15.5 us (4%)
  between operations  13.9 us (4%)
  other arithmetic  12.5 us (3%)
    all_gather x1, waiting for transfers between devices, body(): lax.all_gather(adjoint, 'inst', axis=0, tiled=True)  190 us
    all_to_all x1, blocking collectives, body(): lax.all_to_all(result, 'space', split_axis=1, concat_axis=2, tiled=True)  41.2 us
    all_to_all x1, waiting for transfers between devices, body(): lax.all_to_all(pre, 'space', split_axis=2, concat_axis=1, tiled=True)  33.9 us
    dot_general x1, matrix products, body(): jnp.tensordot(column, lax.all_gather(adjoint, 'inst', axis=0, tiled=True)...  19.2 us
    dot_general x1, matrix products, body(): jnp.einsum('gf,gtrx->ftrx', coupling, center, precision=lax.Precision.HIG...  8.9 us
    ppermute x1, starting transfers between devices, with_halo(): lax.ppermute(lax.slice_in_dim(block, 0, width, axis=dim), axis, backward)  7.93 us
    all_to_all x1, starting transfers between devices, body(): lax.all_to_all(pre, 'space', split_axis=2, concat_axis=1, tiled=True)  7.57 us
  transfers between devices with their start and end apart: 4, of which 2 were waited for; matrix products, arithmetic and copies ran while one was open for 6% of the time, Pallas kernels for 0%

commit v1 on v0

--- a/solution.py
+++ b/solution.py
@@ -2,6 +2,11 @@
 import jax.numpy as jnp
 from jax import lax
 from jax.sharding import PartitionSpec as P
+
+
+def all_by_exchange(value, axis, along):
+    repeated = jnp.stack([value] * lax.axis_size(axis))
+    return jnp.concatenate(lax.all_to_all(repeated, axis, 0, 0), axis=along)
 
 
 def with_halo(block, sides, width):
@@ -92,10 +97,7 @@
     center = adjoint[0]
     column = lax.dynamic_slice_in_dim(matrix, own_slot, 1, 1)[:, 0]
     spectral = jnp.tensordot(
-        column,
-        lax.all_gather(adjoint, "inst", axis=0, tiled=True),
-        axes=1,
-        precision=lax.Precision.HIGHEST,
+        column, all_by_exchange(adjoint, "inst", 0), axes=1, precision=lax.Precision.HIGHEST
     )
     stacked = jnp.concatenate([center, viscosity[None]], axis=0)
     padded = with_halo(stacked, (("space", 1),), 1)

time: 368 us -> 297 us (0.81)
  the two profiles are of different devices: /device:TPU:4 before, /device:TPU:1 now
where the time goes in v1:
time: 297 us; the launch traced here: 293 us
  waiting for transfers between devices  155 us (52%)
  blocking collectives  40.4 us (14%)
  matrix products  39.7 us (13%)
  starting transfers between devices  23.5 us (8%)
  local copies, waits for them, and re-layouts  21.9 us (7%)
  other arithmetic  11.9 us (4%)
    ppermute x1, waiting for transfers between devices, with_halo(): lax.ppermute(lax.slice_in_dim(block, block.shape[dim] - width, None, axis...  71.7 us
    all_to_all x1, waiting for transfers between devices, all_by_exchange(): return jnp.concatenate(lax.all_to_all(repeated, axis, 0, 0), axis=along)  48.6 us
    all_to_all x1, blocking collectives, body(): lax.all_to_all(result, 'space', split_axis=1, concat_axis=2, tiled=True)  40.4 us
    all_to_all x1, waiting for transfers between devices, body(): lax.all_to_all(pre, 'space', split_axis=2, concat_axis=1, tiled=True)  33.4 us
    dot_general x1, matrix products, body(): jnp.tensordot(column, all_by_exchange(adjoint, 'inst', 0), axes=1, precis...  18.9 us
    all_to_all x1, starting transfers between devices, body(): lax.all_to_all(pre, 'space', split_axis=2, concat_axis=1, tiled=True)  13.9 us
    dot_general x1, matrix products, body(): jnp.einsum('gf,gtrx->ftrx', coupling, center, precision=lax.Precision.HIG...  8.9 us
    another operation x1, local copies, waits for them, and re-layouts, all_by_exchange(): repeated = jnp.stack([value] * lax.axis_size(axis))  6.51 us
  transfers between devices with their start and end apart: 4, of which 4 were waited for; matrix products, arithmetic and copies ran while one was open for 7% of the time, Pallas kernels for 0%

profile of v1, /device:TPU:1, one launch (start us, length us, event | category | flops | bytes accessed | tf_op | source)
XLA Modules:
  0.0 292.6 jit_solution(18071329105246955393)
XLA Ops:
  0.0 0.0 copy-start
  0.0 6.5 %stack.2 = f32[8,1,5,8,64,128]{5,4,3,2,1,0:T(8,128)} broadcast(f32[5,8,64,128]{3,2,1,0:T(8,128)} %bitcast.94), dimensions={2,3,4,5} | broadcast | bytes 11796480 | tf_op jit(solution)/shard_map/stack | solution.py:8
  6.5 0.0 copy-start.1
  6.5 0.0 copy-start.2
  6.5 6.0 %all-to-all-start = ((f32[8,1,5,8,64,128]{5,4,3,2,1,0:T(8,128)}), f32[8,1,5,8,64,128]{5,4,3,2,1,0:T(8,128)}, u32[]{:S(2)}, u32[]{:S(2)}) async-start(f32[8,1,5,8,64,128]{5,4,3,2,1,0:T(8,128)} %stack.2), calls=%async_computation | async-start | bytes 20971520 | tf_op jit(solution)/shard_map/all_to_all | solution.py:9
  12.5 0.0 copy-done.1
  12.5 0.0 copy-done.2
  12.5 0.8 fusion.36
  13.3 3.6 %collective-permute-start.1 = (f32[6,1,64,128]{3,2,1,0:T(8,128)}, f32[6,1,64,128]{3,2,1,0:T(8,128)}, u32[]{:S(2)}, u32[]{:S(2)}) collective-permute-start(f32[6,1,64,128]{3,2,1,0:T(8,128)} %get-tuple-element.8), channel_id=1, source_target_pairs={{0,1},{1,2},{2,3},{3,4},{4,5},{5,6},{6,7},{7,8},{8,9},{9,10},{10,1... | collective-permute-start | bytes 589832 | tf_op jit(solution)/shard_map/ppermute | solution.py:18
  16.9 0.0 collective-permute-start
  16.9 0.8 copy.126
  17.7 0.8 slice.88
  18.5 1.9 fusion.78
  20.4 0.0 copy-start.12
  20.4 1.1 copy.108
  21.5 1.1 copy.109
  22.6 1.2 pad_maximum_fusion
  23.8 0.0 copy-done.12
  23.9 0.1 slice_multiply_fusion.2
  23.9 0.0 copy-done.3
  23.9 0.1 add_multiply_fusion
  24.1 1.6 fusion.14
  25.7 2.0 fusion.2
  27.7 3.9 %slice_multiply_fusion.1 = (f32[5,8,64,1]{3,0,2,1:T(8,128)}, f32[5,8,64,1]{3,0,2,1:T(8,128)}) fusion(f32[5,8,64,128]{3,0,2,1:T(8,128)S(1)} %bitcast.93, f32[8,64]{1,0:T(8,128)S(1)} %bitcast.110, f32[5]{0:T(128)S(1)} %get-tuple-element.15, f32[8,64]{1,0:T(8,128)S(1)} %bitcast.111, f32[5]{0:T(128)S(1)} %get-tuple-element.14), kind=kLoop, calls=%fused_computation.6 | loop fusion | flops 10240 | bytes 45096 | tf_op jit(solution)/shard_map/mul | solution.py:86
  31.7 0.0 copy-done.11
  31.7 0.1 fusion.47
  31.8 71.7 %collective-permute-done.1 = f32[6,1,64,128]{3,2,1,0:T(8,128)} collective-permute-done((f32[6,1,64,128]{3,2,1,0:T(8,128)}, f32[6,1,64,128]{3,2,1,0:T(8,128)}, u32[]{:S(2)}, u32[]{:S(2)}) %collective-permute-start.1) | collective-permute-done | bytes 196640 | tf_op jit(solution)/shard_map/ppermute | solution.py:18
  103.5 1.0 copy_dynamic-update-slice_fusion.1
  104.5 0.9 copy_dynamic-update-slice_fusion
  105.5 0.0 copy-start.10
  105.5 0.3 slice.100
  105.7 0.9 collective-permute-done
  106.6 0.8 add_multiply_fusion.2
  107.4 0.0 copy-done.10
  107.4 1.1 fusion.22
  108.5 48.6 %all-to-all-done = f32[8,1,5,8,64,128]{5,4,3,2,1,0:T(8,128)} async-done(((f32[8,1,5,8,64,128]{5,4,3,2,1,0:T(8,128)}), f32[8,1,5,8,64,128]{5,4,3,2,1,0:T(8,128)}, u32[]{:S(2)}, u32[]{:S(2)}) %all-to-all-start) | async-done | bytes 10485792 | tf_op jit(solution)/shard_map/all_to_all | solution.py:9
  157.2 0.0 copy-start.9
  157.2 0.0 copy-start.13
  157.2 18.9 %fusion = f32[1,5,8,64,128]{4,0,3,2,1:T(1,128)S(1)} fusion(f32[8,5,8,64,128]{4,3,2,1,0:T(8,128)} %bitcast.18, f32[8,8]{0,1:T(8,128)S(1)} %fusion.47, s32[]{:T(128)S(6)} %select_n.41), kind=kOutput, calls=%fused_computation | convolution fusion | flops 31457280 | bytes 11796996 | tf_op jit(solution)/shard_map/dot_general | solution.py:99
  176.1 0.0 copy-done
  176.2 0.0 copy-done.4
  176.2 0.0 copy-done.5
  176.2 0.0 copy-done.6
  176.2 0.0 copy-done.7
  176.2 0.0 copy-done.9
  176.2 0.0 copy-done.13
  176.2 8.9 %fusion.13 = f32[5,8,64,128]{3,0,2,1:T(8,128)S(1)} fusion(f32[6,9,64,128]{3,0,2,1:T(8,128)} %copy-done.10, f32[1,5,8,64,128]{4,0,3,2,1:T(1,128)S(1)} %fusion, f32[5,8,64,128]{3,2,1,0:T(8,128)S(1)} %fusion.22, f32[1,5,8,64,128]{4,3,2,1,0:T(8,128)S(1)} %copy-done.9, f32[5,8,64,1]{3,0,2,1:T(8,128)S(1)} %copy-done.6, f32[5,8,64,1]{3,0,2,1:T(8,128)S(1)} %copy-done.5, ...), kind=kOutput, calls=%fused_computation.20 | convolution fusion | flops 24576000 | bytes 17830912 | tf_op jit(solution)/shard_map/gf,gtrx->ftrx/dot_general | solution.py:115
  185.1 1.8 copy.84
  186.9 13.9 %all-to-all-start.1 = ((f32[5,8,64,128]{3,1,0,2:T(8,128)}), f32[5,8,64,128]{3,1,0,2:T(8,128)S(1)}, u32[]{:S(2)}, u32[]{:S(2)}) async-start(f32[5,8,64,128]{3,1,0,2:T(8,128)} %copy.84), calls=%async_computation.1 | async-start | bytes 2621440 | tf_op jit(solution)/shard_map/all_to_all | solution.py:119
  200.9 0.1 compare_select_fusion
  201.0 33.4 %all-to-all-done.1 = f32[5,8,64,128]{3,1,0,2:T(8,128)S(1)} async-done(((f32[5,8,64,128]{3,1,0,2:T(8,128)}), f32[5,8,64,128]{3,1,0,2:T(8,128)S(1)}, u32[]{:S(2)}, u32[]{:S(2)}) %all-to-all-start.1) | async-done | bytes 1310752 | tf_op jit(solution)/shard_map/all_to_all | solution.py:119
  234.4 1.2 copy.127
  235.6 3.2 %fusion.16 = f32[5,256,2,128]{1,3,2,0:T(8,128)S(1)} fusion(f32[256,2]{0,1:T(2,128)S(1)} %compare_select_fusion, f32[5,32,8,2,128]{4,2,0,3,1:T(8,128)S(1)} %bitcast.104), kind=kOutput, calls=%fused_computation.32 | convolution fusion | flops 1007878144 | bytes 2623488 | tf_op jit(solution)/shard_map/tk,ftrx->fkrx/dot_general | solution.py:54
  238.7 4.2 %fusion.15 = f32[5,256,2,128]{1,3,2,0:T(8,128)} fusion(f32[256,2]{0,1:T(2,128)S(1)} %compare_select_fusion, f32[5,32,8,2,128]{4,2,0,3,1:T(8,128)S(1)} %bitcast.105), kind=kOutput, calls=%fused_computation.30 | convolution fusion | flops 1007878144 | bytes 2623488 | tf_op jit(solution)/shard_map/tk,ftrx->fkrx/dot_general | solution.py:55
  242.9 1.7 copy.90
  244.7 0.0 copy-start.8
  244.7 2.2 fusion.30
  246.9 0.0 copy-done.8
  246.9 2.3 fusion.20
  249.2 1.3 copy.91
  250.4 40.4 %all_to_all.38 = f32[5,256,2,128]{3,2,0,1:T(2,128)S(1)} all-to-all(f32[5,256,2,128]{3,2,0,1:T(2,128)S(1)} %copy.91), channel_id=1, replica_groups=mesh['inst'=8,'space'=32] {'space'}, dimensions={1} | all-to-all | bytes 2621440 | tf_op jit(solution)/shard_map/all_to_all | solution.py:122
  290.8 0.1 copy.128
  291.0 0.1 copy.93
  291.1 1.3 copy.94
  (13 shorter events, 0.1 us)
Async XLA Ops:
  0.0 176.1 %copy-start = (f32[5,5]{1,0:T(8,128)S(1)}, f32[5,5]{1,0:T(8,128)}, u32[]{:S(2)}) copy-start(f32[5,5]{1,0:T(8,128)} %param.11) | copy-start | bytes 304
  6.5 6.0 %copy-start.1 = (f32[1,5,8,64,128]{4,3,2,1,0:T(8,128)S(1)}, f32[1,5,8,64,128]{4,3,2,1,0:T(8,128)}, u32[]{:S(2)}) copy-start(f32[1,5,8,64,128]{4,3,2,1,0:T(8,128)} %param.7) | copy-start | bytes 3932164
  6.5 6.0 %copy-start.2 = (f32[8,64,128]{2,1,0:T(8,128)S(1)}, f32[8,64,128]{2,1,0:T(8,128)}, u32[]{:S(2)}) copy-start(f32[8,64,128]{2,1,0:T(8,128)} %param.9) | copy-start | bytes 786436
  6.5 150.6 %all-to-all-start = ((f32[8,1,5,8,64,128]{5,4,3,2,1,0:T(8,128)}), f32[8,1,5,8,64,128]{5,4,3,2,1,0:T(8,128)}, u32[]{:S(2)}, u32[]{:S(2)}) async-start(f32[8,1,5,8,64,128]{5,4,3,2,1,0:T(8,128)} %stack.2), calls=%async_computation | async-start | bytes 20971520 | tf_op jit(solution)/shard_map/all_to_all | solution.py:9
  13.3 90.2 %collective-permute-start.1 = (f32[6,1,64,128]{3,2,1,0:T(8,128)}, f32[6,1,64,128]{3,2,1,0:T(8,128)}, u32[]{:S(2)}, u32[]{:S(2)}) collective-permute-start(f32[6,1,64,128]{3,2,1,0:T(8,128)} %get-tuple-element.8), channel_id=1, source_target_pairs={{0,1},{1,2},{2,3},{3,4},{4,5},{5,6},{6,7},{7,8},{8,9},{9,10},{10,1... | collective-permute-start | bytes 589832 | tf_op jit(solution)/shard_map/ppermute | solution.py:18
  16.9 89.7 %collective-permute-start = (f32[6,1,64,128]{3,2,1,0:T(8,128)}, f32[6,1,64,128]{3,2,1,0:T(8,128)}, u32[]{:S(2)}, u32[]{:S(2)}) collective-permute-start(f32[6,1,64,128]{3,2,1,0:T(8,128)} %get-tuple-element.7), channel_id=1, source_target_pairs={{1,0},{2,1},{3,2},{4,3},{5,4},{6,5},{7,6},{8,7},{9,8},{10,9},{11,1... | collective-permute-start | bytes 589832 | tf_op jit(solution)/shard_map/ppermute | solution.py:21
  20.4 3.4 %copy-start.12 = (s32[5,3]{0,1:T(4,128)S(1)}, s32[5,3]{0,1:T(4,128)}, u32[]{:S(2)}) copy-start(s32[5,3]{0,1:T(4,128)} %param.12) | copy-start | bytes 184
  22.6 1.4 copy-start.3
  27.7 3.9 %copy-start.11 = (s32[8]{0:T(128)S(1)}, s32[8]{0:T(128)}, u32[]{:S(2)}) copy-start(s32[8]{0:T(128)} %param.13) | copy-start | bytes 100
  105.5 2.0 copy-start.10
  157.2 19.0 %copy-start.4 = (f32[5,8,64,127]{3,0,2,1:T(8,128)S(1)}, f32[5,8,64,127]{3,0,2,1:T(8,128)}, u32[]{:S(2)}) copy-start(f32[5,8,64,127]{3,0,2,1:T(8,128)} %fusion.2) | copy-start | bytes 3901444
  157.2 19.0 %copy-start.5 = (f32[5,8,64,1]{3,0,2,1:T(8,128)S(1)}, f32[5,8,64,1]{3,0,2,1:T(8,128)}, u32[]{:S(2)}) copy-start(f32[5,8,64,1]{3,0,2,1:T(8,128)} %get-tuple-element.5) | copy-start | bytes 30724
  157.2 19.0 %copy-start.6 = (f32[5,8,64,1]{3,0,2,1:T(8,128)S(1)}, f32[5,8,64,1]{3,0,2,1:T(8,128)}, u32[]{:S(2)}) copy-start(f32[5,8,64,1]{3,0,2,1:T(8,128)} %get-tuple-element.6) | copy-start | bytes 30724
  157.2 19.0 %copy-start.7 = (f32[5,8,63,128]{3,0,2,1:T(8,128)S(1)}, f32[5,8,63,128]{3,0,2,1:T(8,128)}, u32[]{:S(2)}) copy-start(f32[5,8,63,128]{3,0,2,1:T(8,128)} %fusion.14) | copy-start | bytes 3870724
  157.2 19.0 %copy-start.9 = (f32[1,5,8,64,128]{4,3,2,1,0:T(8,128)S(1)}, f32[1,5,8,64,128]{4,3,2,1,0:T(8,128)}, u32[]{:S(2)}) copy-start(f32[1,5,8,64,128]{4,3,2,1,0:T(8,128)} %param.8) | copy-start | bytes 3932164
  157.2 19.0 %copy-start.13 = (f32[5]{0:T(128)S(1)}, f32[5]{0:T(128)}, u32[]{:S(2)}) copy-start(f32[5]{0:T(128)} %param.10) | copy-start | bytes 64
  186.9 47.5 %all-to-all-start.1 = ((f32[5,8,64,128]{3,1,0,2:T(8,128)}), f32[5,8,64,128]{3,1,0,2:T(8,128)S(1)}, u32[]{:S(2)}, u32[]{:S(2)}) async-start(f32[5,8,64,128]{3,1,0,2:T(8,128)} %copy.84), calls=%async_computation.1 | async-start | bytes 2621440 | tf_op jit(solution)/shard_map/all_to_all | solution.py:119
  244.7 2.2 copy-start.8
